TPU v7x, 32 devices: a whole 2x2x4 slice. The times are simulated.
32 devices in a mesh: visit: 2 (over core), tx: 4 (over y, x), ty: 4 (over z).
Axes of the slice: x: 2, y: 2, z: 4, core: 2. Of those that a mesh axis runs over, the one named last changes fastest.
Arguments:
- raw: bfloat16 [4, 2048, 2048], P('visit', ('tx', 'ty')), may hold values from -12 to 12, as said below
- dark: float32 [2048, 2048], P(('tx', 'ty')), may hold values from 0 to 0.8
- flat: float32 [2048, 2048], P(('tx', 'ty')), may hold values from 0.5 to 1.5
- mask: int32 [4, 2048, 2048], P('visit', ('tx', 'ty')), may hold values 0 or 1
- offsets: int32 [4, 2], P('visit'), may hold values from 0 to 255
- scales: float32 [4, 2], P('visit'), may hold values from 0.985 to 1.015
- fracs: float32 [4, 2], P('visit'), may hold values from 0 to 1
Outputs:
- coadd: float32 [2048, 2048], P('visit', ('tx', 'ty'))
Inputs may be any that keep to these rules, and one draw needn't show every extreme that they name: `raw`: each exposure's pixels have a noise level of its own.
All inputs are finite; a program needn't handle non-finite values. No bound on the sum of `mask` on one device may be relied on, other than what follows from the above.
Results may differ from a plain program's by a relative error of at most 0.00145.
The roundings to bfloat16 on the way count: a program that leaves them out, or rounds other values in their place, can miss the bound.
Values may be sent and summed in bfloat16 or wider, within the bound.
A program may use at most 64 MiB of HBM per device.

v0:
```python
import functools

import jax
import jax.numpy as jnp
from jax import lax
from jax.experimental import pallas as pl
from jax.experimental.pallas import tpu as pltpu
from jax.sharding import PartitionSpec as P

MESH = pl.DeviceIdType.MESH
COL_WINDOW = 640
COL_ALIGN = 128
ROW_WINDOW = 512
ROW_ALIGN = 64


def lanczos(offsets_t):
    return jnp.where(jnp.abs(offsets_t) < 3.0, jnp.sinc(offsets_t) * jnp.sinc(offsets_t / 3.0), 0.0)


def banded(taps, first, window):
    frame = (lax.broadcasted_iota(jnp.int32, (window, taps.shape[1]), 0) + first).astype(jnp.float32)
    step = frame - taps[6:7, :]
    total = jnp.zeros_like(step)
    for tap in range(6):
        total = jnp.where(step == float(tap - 2), taps[tap : tap + 1, :], total)
    return total.astype(jnp.bfloat16)


def window_start(sky, frame_len, window, align):
    lowest = lax.div(lax.max((sky - 255) * 197 - 800, 0), 200)
    return pl.multiple_of(lax.min(lax.div(lowest, align) * align, frame_len - window), align)


def kernel(dims, raw, dark, flat, mask, taps, out, image, outgoing, stats, totals, partial, *rest):
    exposures, parts, band, frame_len, visits, n_tx, n_ty = dims
    strips = rest[:exposures]
    send_sem, recv_sem, stat_send, stat_recv, sum_send, sum_recv = rest[exposures:]
    width = frame_len // parts
    vi, ti, yi = lax.axis_index("visit"), lax.axis_index("tx"), lax.axis_index("ty")
    me = ti * n_ty + yi

    def peer(step):
        to = lax.rem(me + step, parts)
        return to, (vi, lax.div(to, n_ty), lax.rem(to, n_ty))

    barrier = pltpu.get_barrier_semaphore()

    def greet(step, carry):
        pl.semaphore_signal(barrier, inc=1, device_id=peer(step)[1], device_id_type=MESH)
        return carry

    def greet_visit(step, carry):
        to = (lax.rem(vi + step, visits), ti, yi)
        pl.semaphore_signal(barrier, inc=1, device_id=to, device_id_type=MESH)
        return carry

    lax.fori_loop(1, parts, greet, 0)
    lax.fori_loop(1, visits, greet_visit, 0)

    def correct(expo):
        def chunk(at, carry):
            sumsq, count = carry
            cols = pl.ds(pl.multiple_of(at * 128, 128), 128)
            good = mask[expo, :, cols].astype(jnp.float32)
            fixed = (raw[expo, :, cols].astype(jnp.float32) - dark[:, cols]) * flat[:, cols] * good
            image[expo, 0:band, cols] = fixed.astype(jnp.bfloat16)
            image[expo, band : 2 * band, cols] = good.astype(jnp.bfloat16)
            sumsq = sumsq + jnp.sum(fixed * fixed, axis=0, keepdims=True)
            count = count + jnp.sum(good, axis=0, keepdims=True)
            return sumsq, count

        zero = jnp.zeros((1, 128), jnp.float32)
        sumsq, count = lax.fori_loop(0, frame_len // 128, chunk, (zero, zero))
        stats[me, expo : expo + 1, :] = sumsq
        stats[me, exposures + expo : exposures + expo + 1, :] = count

    def strip_copy(expo, step):
        return pltpu.make_async_remote_copy(
            src_ref=outgoing.at[expo, step],
            dst_ref=strips[expo].at[pl.ds(pl.multiple_of(me * band, band), band), :],
            send_sem=send_sem.at[expo, step],
            recv_sem=recv_sem.at[expo, step],
            device_id=peer(step)[1],
            device_id_type=MESH,
        )

    def stat_copy(step):
        return pltpu.make_async_remote_copy(
            src_ref=stats.at[me],
            dst_ref=stats.at[me],
            send_sem=stat_send.at[step],
            recv_sem=stat_recv.at[step],
            device_id=peer(step)[1],
            device_id_type=MESH,
        )

    def column(expo, step):
        to, _ = peer(step)
        first = window_start(to * width, frame_len, COL_WINDOW, COL_ALIGN)
        cols = pl.ds(pl.multiple_of(to * width, width), width)
        k = banded(taps[expo, 1, :, cols], first, COL_WINDOW)
        operand = image[expo, :, pl.ds(first, COL_WINDOW)]
        return jnp.dot(operand, k, preferred_element_type=jnp.float32).astype(jnp.bfloat16)

    for expo in range(exposures):
        correct(expo)
        if expo == 0:
            pl.semaphore_wait(barrier, parts + visits - 2)

        def send_step(step, carry, expo=expo):
            both = column(expo, step)
            outgoing[expo, step, :, 0:width] = both[0:band]
            outgoing[expo, step, :, width : 2 * width] = both[band : 2 * band]
            strip_copy(expo, step).start()
            return carry

        lax.fori_loop(1, parts, send_step, 0)
        both = column(expo, 0)
        rows = pl.ds(pl.multiple_of(me * band, band), band)
        strips[expo][rows, 0:width] = both[0:band]
        strips[expo][rows, width : 2 * width] = both[band : 2 * band]

    def send_stat(step, carry):
        stat_copy(step).start()
        return carry

    lax.fori_loop(1, parts, send_stat, 0)

    def wait_stat(step, carry):
        stat_copy(step).wait()
        return carry

    lax.fori_loop(1, parts, wait_stat, 0)
    lanes = jnp.sum(stats[...], axis=0)
    sums = jnp.sum(lanes, axis=1, keepdims=True)

    own = frame_len // visits
    blocks = own // 128

    def sum_copy(step, block):
        to = lax.rem(vi + step, visits)
        at = pl.multiple_of(to * own + block * 128, 128)
        return pltpu.make_async_remote_copy(
            src_ref=totals.at[pl.ds(at, 128), :],
            dst_ref=partial.at[step, pl.ds(pl.multiple_of(block * 128, 128), 128), :],
            send_sem=sum_send.at[step, block],
            recv_sem=sum_recv.at[step, block],
            device_id=(to, ti, yi),
            device_id_type=MESH,
        )

    for expo in range(exposures):

        def wait_strip(step, carry, expo=expo):
            strip_copy(expo, step).wait()
            return carry

        lax.fori_loop(1, parts, wait_strip, 0)
        count = sums[exposures + expo : exposures + expo + 1, :]
        weight = count / (sums[expo : expo + 1, :] + 1e-05 * count)

        def row(at, expo=expo, weight=weight):
            at = pl.multiple_of(at, 128)
            first = window_start(at, frame_len, ROW_WINDOW, ROW_ALIGN)
            k = banded(taps[expo, 0, :, pl.ds(at, 128)], first, ROW_WINDOW)
            operand = strips[expo][pl.ds(first, ROW_WINDOW), :]
            dims_of = (((0,), (0,)), ((), ()))
            warped = weight * lax.dot_general(k, operand, dims_of, preferred_element_type=jnp.float32)
            rows = pl.ds(at, 128)
            totals[rows, :] = warped if expo == 0 else totals[rows, :] + warped

        last = expo == exposures - 1

        def row_step(index, carry, row=row, last=last):
            step, block = lax.div(index, blocks) + 1, lax.rem(index, blocks)
            row(lax.rem(vi + step, visits) * own + block * 128)
            if last:
                sum_copy(step, block).start()
            return carry

        def own_step(block, carry, row=row):
            row(vi * own + block * 128)
            return carry

        lax.fori_loop(0, (visits - 1) * blocks, row_step, 0)
        lax.fori_loop(0, blocks, own_step, 0)

    def finish(block, carry):
        rows = pl.ds(pl.multiple_of(block * 128, 128), 128)
        total = totals[pl.ds(pl.multiple_of(vi * own + block * 128, 128), 128), :]
        for step in range(1, visits):
            sum_copy(step, block).wait()
            total = total + partial[step, rows, :]
        out[rows, :] = total[:, 0:width] / jnp.maximum(total[:, width : 2 * width], 1.0)
        return carry

    lax.fori_loop(0, blocks, finish, 0)


def shards(n_visit, n_tx, n_ty, raw, dark, flat, mask, offsets, scales, fracs):
    exposures, band, frame_len = raw.shape
    parts = n_tx * n_ty
    width = frame_len // parts
    sky = jnp.arange(frame_len, dtype=jnp.float32)
    coords = (sky - offsets[..., None].astype(jnp.float32)) * scales[..., None] + fracs[..., None]
    base = jnp.floor(coords)
    near = jnp.arange(-2, 4, dtype=jnp.float32)[:, None]
    taps = lanczos(coords[:, :, None, :] - (base[:, :, None, :] + near))
    taps = taps.astype(jnp.bfloat16).astype(jnp.float32)
    taps = jnp.concatenate([taps, base[:, :, None, :], base[:, :, None, :]], axis=2)
    own = frame_len // n_visit
    vmem = pl.BlockSpec(memory_space=pltpu.VMEM)
    dims = (exposures, parts, band, frame_len, n_visit, n_tx, n_ty)
    dma = pltpu.SemaphoreType.DMA
    return pl.pallas_call(
        functools.partial(kernel, dims),
        out_shape=jax.ShapeDtypeStruct((own, width), jnp.float32),
        in_specs=[vmem] * 5,
        out_specs=vmem,
        scratch_shapes=[
            pltpu.VMEM((exposures, 2 * band, frame_len), jnp.bfloat16),
            pltpu.VMEM((exposures, parts, band, 2 * width), jnp.bfloat16),
            pltpu.VMEM((parts, 2 * exposures, 128), jnp.float32),
            pltpu.VMEM((frame_len, 2 * width), jnp.float32),
            pltpu.VMEM((n_visit, own, 2 * width), jnp.float32),
        ]
        + [pltpu.VMEM((frame_len, 2 * width), jnp.bfloat16)] * exposures
        + [
            dma((exposures, parts)),
            dma((exposures, parts)),
            dma((parts,)),
            dma((parts,)),
            dma((n_visit, own // 128)),
            dma((n_visit, own // 128)),
        ],
        compiler_params=pltpu.CompilerParams(
            collective_id=0, has_side_effects=True, vmem_limit_bytes=60000000
        ),
    )(raw, dark, flat, mask, taps)


def solution(mesh):
    in_specs = (
        P("visit", ("tx", "ty"), None),
        P(("tx", "ty"), None),
        P(("tx", "ty"), None),
        P("visit", ("tx", "ty"), None),
        P("visit", None),
        P("visit", None),
        P("visit", None),
    )
    out_specs = P("visit", ("tx", "ty"))
    body = functools.partial(shards, mesh.shape["visit"], mesh.shape["tx"], mesh.shape["ty"])
    return jax.shard_map(body, mesh=mesh, in_specs=in_specs, out_specs=out_specs, check_vma=False)
```

profile of v0, /device:TPU:0, one launch (start us, length us, event | category | flops | bytes accessed | tf_op | source)
XLA Modules:
  0.0 76.0 jit_solution(571459442827183499)
XLA Ops:
  0.0 0.7 convert_element_type.13
  0.7 0.8 %add_floor_fusion = f32[2,2,1,2048]{3,2,1,0:T(1,128)S(1)} fusion(f32[2,2]{1,0:T(2,128)} %param.14, f32[2,2]{1,0:T(2,128)} %param.13, f32[2,2]{1,0:T(2,128)S(1)} %convert_element_type.13), kind=kLoop, calls=%fused_computation.56 | loop fusion | flops 32768 | bytes 32816 | tf_op jit(solution)/shard_map/floor | solution.py:207
  1.5 0.8 %multiply_add_fusion.2 = (f32[2,2,2048]{2,1,0:T(2,128)S(1)}, f32[2,2,2048]{2,1,0:T(2,128)S(1)}) fusion(f32[2,2]{1,0:T(2,128)} %param.14, f32[2,2]{1,0:T(2,128)} %param.13, f32[2,2]{1,0:T(2,128)S(1)} %convert_element_type.13), kind=kLoop, calls=%fused_computation.57 | loop fusion | flops 32768 | bytes 65584 | tf_op jit(solution)/shard_map/add | solution.py:206
  2.3 0.7 fusion.31
  3.0 0.8 %pad_maximum_fusion.taps = f32[2,2,8,2048]{3,2,1,0:T(8,128)} fusion(f32[2,2,1,2048]{3,2,1,0:T(1,128)S(1)} %add_floor_fusion, f32[2,2,6,2048]{3,2,1,0:T(8,128)S(1)} %fusion.31), kind=kLoop, calls=%fused_computation.30 | loop fusion | flops 131072 | bytes 491520 | tf_op jit(solution)/shard_map/concatenate | solution.py:211
  3.8 70.3 %shard_map.73 = f32[1024,128]{1,0:T(8,128)} custom-call(bf16[2,128,2048]{2,1,0:T(8,128)(2,1)} %raw.1, f32[128,2048]{1,0:T(8,128)} %dark.1, f32[128,2048]{1,0:T(8,128)} %flat.1, s32[2,128,2048]{2,1,0:T(8,128)} %mask.1, f32[2,2,8,2048]{3,2,1,0:T(8,128)} %pad_maximum_fusion.taps), custom_call_target="tpu_custom_call" | custom-call | tf_op jit(solution)/shard_map/pallas_call | solution.py:216
  74.1 1.9 %copy.9 = f32[1024,128]{1,0:T(8,128)} copy(f32[1024,128]{1,0:T(8,128)} %shard_map.73) | data formatting | bytes 1048576
  (1 shorter events, 0.0 us)
where the time goes:
time: 76.2 us; the launch traced here: 76 us
  Pallas kernels  70.3 us (92%)
  other arithmetic  3.76 us (5%)
  local copies, waits for them, and re-layouts  1.87 us (2%)
    pallas_call x1, Pallas kernels, shards(): pl.pallas_call(functools.partial(kernel, dims), out_shape=jax.ShapeDtypeS...  70.3 us
    unnamed x1, local copies, waits for them, and re-layouts  1.87 us

commit v1 on v0

--- a/solution.py
+++ b/solution.py
@@ -14,8 +14,13 @@
 ROW_ALIGN = 64
 
 
-def lanczos(offsets_t):
-    return jnp.where(jnp.abs(offsets_t) < 3.0, jnp.sinc(offsets_t) * jnp.sinc(offsets_t / 3.0), 0.0)
+def sinc(t):
+    at = jnp.pi * jnp.where(t == 0.0, 1.0, t)
+    return jnp.where(t == 0.0, 1.0, jnp.sin(at) / at)
+
+
+def lanczos(t):
+    return jnp.where(jnp.abs(t) < 3.0, sinc(t) * sinc(t / 3.0), 0.0)
 
 
 def banded(taps, first, window):
@@ -32,17 +37,31 @@
     return pl.multiple_of(lax.min(lax.div(lowest, align) * align, frame_len - window), align)
 
 
-def kernel(dims, raw, dark, flat, mask, taps, out, image, outgoing, stats, totals, partial, *rest):
+def kernel(dims, offsets, scales, fracs, raw_in, dark_in, flat_in, mask_in, out, *scratch):
     exposures, parts, band, frame_len, visits, n_tx, n_ty = dims
-    strips = rest[:exposures]
-    send_sem, recv_sem, stat_send, stat_recv, sum_send, sum_recv = rest[exposures:]
+    raw, dark, flat, mask, taps, rowk, image, outgoing, stats, totals, partial = scratch[:11]
+    strips = scratch[11 : 11 + exposures]
+    in_sem, send_sem, recv_sem, stat_send, stat_recv, sum_send, sum_recv = scratch[11 + exposures :]
     width = frame_len // parts
     vi, ti, yi = lax.axis_index("visit"), lax.axis_index("tx"), lax.axis_index("ty")
     me = ti * n_ty + yi
 
+    half = n_ty // 2
+    own_step = parts - 1
+
     def peer(step):
-        to = lax.rem(me + step, parts)
-        return to, (vi, lax.div(to, n_ty), lax.rem(to, n_ty))
+        high, at = 1 - lax.div(step, parts // 2), lax.rem(step, parts // 2)
+        low, over = lax.rem(lax.div(at, n_tx) + 1, half), lax.rem(lax.rem(at, n_tx) + 1, n_tx)
+        to_y = lax.rem(lax.div(yi, half) + high, 2) * half + lax.rem(lax.rem(yi, half) + low, half)
+        to_t = lax.rem(ti + over, n_tx)
+        return to_t * n_ty + to_y, (vi, to_t, to_y)
+
+    loads = [(dark_in, dark), (flat_in, flat)]
+    for expo in range(exposures):
+        loads += [(raw_in.at[expo], raw.at[expo]), (mask_in.at[expo], mask.at[expo])]
+    loads = [pltpu.make_async_copy(src, dst, in_sem.at[n]) for n, (src, dst) in enumerate(loads)]
+    for load in loads:
+        load.start()
 
     barrier = pltpu.get_barrier_semaphore()
 
@@ -55,8 +74,18 @@
         pl.semaphore_signal(barrier, inc=1, device_id=to, device_id_type=MESH)
         return carry
 
-    lax.fori_loop(1, parts, greet, 0)
+    lax.fori_loop(0, own_step, greet, 0)
     lax.fori_loop(1, visits, greet_visit, 0)
+
+    def weigh(expo, axis):
+        shape = (8, frame_len)
+        sky = lax.broadcasted_iota(jnp.int32, shape, 1).astype(jnp.float32)
+        tap = lax.broadcasted_iota(jnp.int32, shape, 0).astype(jnp.float32)
+        offset = offsets[expo, axis].astype(jnp.float32)
+        coords = (sky - offset) * scales[expo, axis] + fracs[expo, axis]
+        base = jnp.floor(coords)
+        values = lanczos(coords - (base + (tap - 2.0)))
+        taps[expo, axis, :, :] = jnp.where(tap < 6.0, values, base)
 
     def correct(expo):
         def chunk(at, carry):
@@ -103,10 +132,23 @@
         operand = image[expo, :, pl.ds(first, COL_WINDOW)]
         return jnp.dot(operand, k, preferred_element_type=jnp.float32).astype(jnp.bfloat16)
 
+    def send_stat(step, carry):
+        stat_copy(step).start()
+        return carry
+
+    weigh(0, 1)
+    loads[0].wait()
+    loads[1].wait()
     for expo in range(exposures):
+        if expo > 0:
+            weigh(expo, 1)
+        loads[2 + 2 * expo].wait()
+        loads[3 + 2 * expo].wait()
         correct(expo)
         if expo == 0:
             pl.semaphore_wait(barrier, parts + visits - 2)
+        if expo == exposures - 1:
+            lax.fori_loop(0, own_step, send_stat, 0)
 
         def send_step(step, carry, expo=expo):
             both = column(expo, step)
@@ -115,25 +157,26 @@
             strip_copy(expo, step).start()
             return carry
 
-        lax.fori_loop(1, parts, send_step, 0)
-        both = column(expo, 0)
+        lax.fori_loop(0, own_step, send_step, 0)
+        both = column(expo, own_step)
         rows = pl.ds(pl.multiple_of(me * band, band), band)
         strips[expo][rows, 0:width] = both[0:band]
         strips[expo][rows, width : 2 * width] = both[band : 2 * band]
 
-    def send_stat(step, carry):
-        stat_copy(step).start()
-        return carry
-
-    lax.fori_loop(1, parts, send_stat, 0)
+    for expo in range(exposures):
+        weigh(expo, 0)
+
+        def build(block, carry, expo=expo):
+            at = pl.multiple_of(block * 128, 128)
+            first = window_start(at, frame_len, ROW_WINDOW, ROW_ALIGN)
+            rowk[expo, pl.ds(at, 128), :] = banded(taps[expo, 0, :, pl.ds(at, 128)], first, ROW_WINDOW).T
+            return carry
+
+        lax.fori_loop(0, frame_len // 128, build, 0)
 
     def wait_stat(step, carry):
         stat_copy(step).wait()
         return carry
-
-    lax.fori_loop(1, parts, wait_stat, 0)
-    lanes = jnp.sum(stats[...], axis=0)
-    sums = jnp.sum(lanes, axis=1, keepdims=True)
 
     own = frame_len // visits
     blocks = own // 128
@@ -156,18 +199,21 @@
             strip_copy(expo, step).wait()
             return carry
 
-        lax.fori_loop(1, parts, wait_strip, 0)
+        lax.fori_loop(0, own_step, wait_strip, 0)
+        if expo == 0:
+            lax.fori_loop(0, own_step, wait_stat, 0)
+            lanes = jnp.sum(stats[...], axis=0)
+            sums = jnp.sum(lanes, axis=1, keepdims=True)
         count = sums[exposures + expo : exposures + expo + 1, :]
         weight = count / (sums[expo : expo + 1, :] + 1e-05 * count)
 
         def row(at, expo=expo, weight=weight):
             at = pl.multiple_of(at, 128)
             first = window_start(at, frame_len, ROW_WINDOW, ROW_ALIGN)
-            k = banded(taps[expo, 0, :, pl.ds(at, 128)], first, ROW_WINDOW)
+            rows = pl.ds(at, 128)
             operand = strips[expo][pl.ds(first, ROW_WINDOW), :]
-            dims_of = (((0,), (0,)), ((), ()))
-            warped = weight * lax.dot_general(k, operand, dims_of, preferred_element_type=jnp.float32)
-            rows = pl.ds(at, 128)
+            k = rowk[expo, rows, :]
+            warped = weight * jnp.dot(k, operand, preferred_element_type=jnp.float32)
             totals[rows, :] = warped if expo == 0 else totals[rows, :] + warped
 
         last = expo == exposures - 1
@@ -179,12 +225,12 @@
                 sum_copy(step, block).start()
             return carry
 
-        def own_step(block, carry, row=row):
+        def own_row(block, carry, row=row):
             row(vi * own + block * 128)
             return carry
 
         lax.fori_loop(0, (visits - 1) * blocks, row_step, 0)
-        lax.fori_loop(0, blocks, own_step, 0)
+        lax.fori_loop(0, blocks, own_row, 0)
 
     def finish(block, carry):
         rows = pl.ds(pl.multiple_of(block * 128, 128), 128)
@@ -202,23 +248,23 @@
     exposures, band, frame_len = raw.shape
     parts = n_tx * n_ty
     width = frame_len // parts
-    sky = jnp.arange(frame_len, dtype=jnp.float32)
-    coords = (sky - offsets[..., None].astype(jnp.float32)) * scales[..., None] + fracs[..., None]
-    base = jnp.floor(coords)
-    near = jnp.arange(-2, 4, dtype=jnp.float32)[:, None]
-    taps = lanczos(coords[:, :, None, :] - (base[:, :, None, :] + near))
-    taps = taps.astype(jnp.bfloat16).astype(jnp.float32)
-    taps = jnp.concatenate([taps, base[:, :, None, :], base[:, :, None, :]], axis=2)
     own = frame_len // n_visit
+    smem = pl.BlockSpec(memory_space=pltpu.SMEM)
     vmem = pl.BlockSpec(memory_space=pltpu.VMEM)
     dims = (exposures, parts, band, frame_len, n_visit, n_tx, n_ty)
     dma = pltpu.SemaphoreType.DMA
     return pl.pallas_call(
         functools.partial(kernel, dims),
         out_shape=jax.ShapeDtypeStruct((own, width), jnp.float32),
-        in_specs=[vmem] * 5,
+        in_specs=[smem] * 3 + [pl.BlockSpec(memory_space=pl.ANY)] * 4,
         out_specs=vmem,
         scratch_shapes=[
+            pltpu.VMEM(raw.shape, raw.dtype),
+            pltpu.VMEM(dark.shape, dark.dtype),
+            pltpu.VMEM(flat.shape, flat.dtype),
+            pltpu.VMEM(mask.shape, mask.dtype),
+            pltpu.VMEM((exposures, 2, 8, frame_len), jnp.float32),
+            pltpu.VMEM((exposures, frame_len, ROW_WINDOW), jnp.bfloat16),
             pltpu.VMEM((exposures, 2 * band, frame_len), jnp.bfloat16),
             pltpu.VMEM((exposures, parts, band, 2 * width), jnp.bfloat16),
             pltpu.VMEM((parts, 2 * exposures, 128), jnp.float32),
@@ -227,6 +273,7 @@
         ]
         + [pltpu.VMEM((frame_len, 2 * width), jnp.bfloat16)] * exposures
         + [
+            dma((2 + 2 * exposures,)),
             dma((exposures, parts)),
             dma((exposures, parts)),
             dma((parts,)),
@@ -237,7 +284,7 @@
         compiler_params=pltpu.CompilerParams(
             collective_id=0, has_side_effects=True, vmem_limit_bytes=60000000
         ),
-    )(raw, dark, flat, mask, taps)
+    )(offsets, scales, fracs, raw, dark, flat, mask)
 
 
 def solution(mesh):

time: 76.2 us -> 62.9 us (0.83)
  Pallas kernels: 70.3 us -> 60.8 us
  other arithmetic: 3.76 us -> 0 us
    pallas_call x1, Pallas kernels: 70.3 us -> 60.8 us  [shards(): pl.pallas_call(functools.partial(kernel, dims), out_shape=jax.ShapeDtypeS...]
    convert_element_type x2 -> x0, other arithmetic: 1.38 us -> none  [the longest x1 0.7 us: shards(): taps = taps.astype(jnp.bfloat16).astype(jnp.float32)]
    floor x1 -> x0, other arithmetic: 0.8 us -> none  [shards(): base = jnp.floor(coords)]
    add x2 -> x0, other arithmetic: 0.8 us -> none  [the longest x1 0.79 us: shards(): (sky - offsets[..., None].astype(jnp.float32)) * scales[..., None]]
    concatenate x1 -> x0, other arithmetic: 0.78 us -> none  [shards(): jnp.concatenate([taps, base[:, :, None, :], base[:, :, None, :]], axis=2)]
where the time goes in v1:
time: 62.9 us; the launch traced here: 62.7 us
  Pallas kernels  60.8 us (97%)
  local copies, waits for them, and re-layouts  1.87 us (3%)
    pallas_call x1, Pallas kernels, shards(): pl.pallas_call(functools.partial(kernel, dims), out_shape=jax.ShapeDtypeS...  60.8 us
    unnamed x1, local copies, waits for them, and re-layouts  1.87 us

profile of v1, /device:TPU:0, one launch (start us, length us, event | category | flops | bytes accessed | tf_op | source)
XLA Modules:
  0.0 62.7 jit_solution(9223946307313504135)
XLA Ops:
  0.0 60.8 %shard_map.73 = f32[1024,128]{1,0:T(8,128)} custom-call(s32[2,2]{1,0:T(2,128)} %offsets.1, f32[2,2]{1,0:T(2,128)} %scales.1, f32[2,2]{1,0:T(2,128)} %fracs.1, bf16[2,128,2048]{2,1,0:T(8,128)(2,1)} %raw_in.1, f32[128,2048]{1,0:T(8,128)} %dark_in.1, f32[128,2048]{1,0:T(8,128)} %flat_in.1, s32[2,128,2048]{2,1,0:T(8,128)} %mask_in.1), custom_call_target="tpu_custom_call" | custom-call | tf_op jit(solution)/shard_map/pallas_call | solution.py:256
  60.9 1.9 %copy.9 = f32[1024,128]{1,0:T(8,128)} copy(f32[1024,128]{1,0:T(8,128)} %shard_map.73) | data formatting | bytes 1048576

commit v2 on v1

--- a/solution.py
+++ b/solution.py
@@ -151,6 +151,7 @@
             lax.fori_loop(0, own_step, send_stat, 0)
 
         def send_step(step, carry, expo=expo):
+            step = lax.rem(step, 2) * (parts // 2) + lax.div(step, 2)
             both = column(expo, step)
             outgoing[expo, step, :, 0:width] = both[0:band]
             outgoing[expo, step, :, width : 2 * width] = both[band : 2 * band]

time: 62.9 us -> 62.8 us (level)
  no operation moved by 1% of the time
where the time goes in v2:
time: 62.8 us; the launch traced here: 62.6 us
  Pallas kernels  60.8 us (97%)
  local copies, waits for them, and re-layouts  1.87 us (3%)
    pallas_call x1, Pallas kernels, shards(): pl.pallas_call(functools.partial(kernel, dims), out_shape=jax.ShapeDtypeS...  60.8 us
    unnamed x1, local copies, waits for them, and re-layouts  1.87 us

profile of v2, /device:TPU:0, one launch (start us, length us, event | category | flops | bytes accessed | tf_op | source)
XLA Modules:
  0.0 62.6 jit_solution(892859304589076653)
XLA Ops:
  0.0 60.8 %shard_map.73 = f32[1024,128]{1,0:T(8,128)} custom-call(s32[2,2]{1,0:T(2,128)} %offsets.1, f32[2,2]{1,0:T(2,128)} %scales.1, f32[2,2]{1,0:T(2,128)} %fracs.1, bf16[2,128,2048]{2,1,0:T(8,128)(2,1)} %raw_in.1, f32[128,2048]{1,0:T(8,128)} %dark_in.1, f32[128,2048]{1,0:T(8,128)} %flat_in.1, s32[2,128,2048]{2,1,0:T(8,128)} %mask_in.1), custom_call_target="tpu_custom_call" | custom-call | tf_op jit(solution)/shard_map/pallas_call | solution.py:257
  60.8 1.9 %copy.9 = f32[1024,128]{1,0:T(8,128)} copy(f32[1024,128]{1,0:T(8,128)} %shard_map.73) | data formatting | bytes 1048576

commit v3 on v2

--- a/solution.py
+++ b/solution.py
@@ -60,7 +60,7 @@
     for expo in range(exposures):
         loads += [(raw_in.at[expo], raw.at[expo]), (mask_in.at[expo], mask.at[expo])]
     loads = [pltpu.make_async_copy(src, dst, in_sem.at[n]) for n, (src, dst) in enumerate(loads)]
-    for load in loads:
+    for load in loads[:4]:
         load.start()
 
     barrier = pltpu.get_barrier_semaphore()
@@ -144,6 +144,8 @@
             weigh(expo, 1)
         loads[2 + 2 * expo].wait()
         loads[3 + 2 * expo].wait()
+        for load in loads[4 + 2 * expo : 6 + 2 * expo]:
+            load.start()
         correct(expo)
         if expo == 0:
             pl.semaphore_wait(barrier, parts + visits - 2)

time: 62.8 us -> 62.8 us (level)
  no operation moved by 1% of the time
where the time goes in v3:
time: 62.8 us; the launch traced here: 62.7 us
  Pallas kernels  60.8 us (97%)
  local copies, waits for them, and re-layouts  1.87 us (3%)
    pallas_call x1, Pallas kernels, shards(): pl.pallas_call(functools.partial(kernel, dims), out_shape=jax.ShapeDtypeS...  60.8 us
    unnamed x1, local copies, waits for them, and re-layouts  1.87 us

profile of v3, /device:TPU:0, one launch (start us, length us, event | category | flops | bytes accessed | tf_op | source)
XLA Modules:
  0.0 62.7 jit_solution(827807881280935018)
XLA Ops:
  0.0 60.8 %shard_map.73 = f32[1024,128]{1,0:T(8,128)} custom-call(s32[2,2]{1,0:T(2,128)} %offsets.1, f32[2,2]{1,0:T(2,128)} %scales.1, f32[2,2]{1,0:T(2,128)} %fracs.1, bf16[2,128,2048]{2,1,0:T(8,128)(2,1)} %raw_in.1, f32[128,2048]{1,0:T(8,128)} %dark_in.1, f32[128,2048]{1,0:T(8,128)} %flat_in.1, s32[2,128,2048]{2,1,0:T(8,128)} %mask_in.1), custom_call_target="tpu_custom_call" | custom-call | tf_op jit(solution)/shard_map/pallas_call | solution.py:259
  60.8 1.9 %copy.9 = f32[1024,128]{1,0:T(8,128)} copy(f32[1024,128]{1,0:T(8,128)} %shard_map.73) | data formatting | bytes 1048576
